TPU v7x, 256 devices: a whole 4x4x8 slice. The times are simulated.
256 devices in a mesh: row: 16 (over z, core), col: 8 (over x, y_lo), vec: 2 (over y_hi).
Axes of the slice: x: 4, y: 4 (y_hi: 2, y_lo: 2; y = y_hi * 2 + y_lo), z: 8, core: 2. Of those that a mesh axis runs over, the one named last changes fastest.
Arguments:
- vectors: bfloat16 [16, 131072], P('vec', ('row', 'col')), may hold values from -6 to 6
- tile_vals: bfloat16 [16, 8, 256, 128, 128], P('row', 'col'), may hold values from -0.09375 to 0.09375
- tile_rows: int32 [16, 8, 256], P('row', 'col'), may hold values from 0 to 1023, as said below
- tile_cols: int32 [16, 8, 256], P('row', 'col'), may hold values from 0 to 1023, as said below
- tile_counts: int32 [16, 8], P('row', 'col'), may hold values from 1 to 256, as said below
Outputs:
- product: bfloat16 [16, 131072], P('vec', ('row', 'col'))
- gram: float32 [16, 16], P(None, 'vec')
Inputs may be any that keep to these rules, and one draw needn't show every extreme that they name: `tile_rows`: list [i, j] names tiles whose row index r has i * 64 <= r < (i + 1) * 64 and whose column index c has (c // 8) % (8) == j, that is the column's block of 8 tile rows, numbered c // 8, is held by column group j; live slots name distinct tiles with r >= c; slots at or beyond the count hold in-range indices that must be ignored. `tile_cols`: see tile_rows; the same slots. `tile_counts`: some lists are full in every draw; lists near the top of the triangle hold few tiles.
All inputs are finite; a program needn't handle non-finite values.
Results may differ from a plain program's by a relative error of at most 0.001.
Values may be sent and summed in bfloat16 or wider, within the bound.
A program may use at most 64 MiB of HBM per device.

v0:
```python
import math
import jax
import jax.numpy as jnp
from jax import lax
from jax.sharding import PartitionSpec as P


def shards(vectors, tile_vals, tile_rows, tile_cols, tile_counts):
    nrow = lax.axis_size("row")
    ncol = lax.axis_size("col")
    vlocal, width = vectors.shape
    tile = tile_vals.shape[-1]
    stretch = width // tile
    span = ncol * stretch
    colspan = nrow * stretch
    row_x = lax.all_gather(vectors, "col", axis=1, tiled=True)
    col_x = lax.all_gather(vectors, "row", axis=1, tiled=True)
    tiles = tile_vals[0, 0]
    rows = tile_rows[0, 0]
    cols = tile_cols[0, 0]
    count = tile_counts[0, 0]
    slots = jnp.arange(rows.shape[0], dtype=jnp.int32)
    live = slots < count
    mirror = live & (rows != cols)
    row_place = rows % span
    col_place = cols // span * stretch + cols % stretch
    row_blocks = row_x.reshape(vlocal, span, tile)
    col_blocks = col_x.reshape(vlocal, colspan, tile)
    picked_cols = jnp.take(col_blocks, col_place, axis=1)
    picked_rows = jnp.take(row_blocks, row_place, axis=1)
    down = jnp.einsum("tij,vtj->vti", tiles, picked_cols, preferred_element_type=jnp.float32)
    upper = jnp.einsum("tij,vti->vtj", tiles, picked_rows, preferred_element_type=jnp.float32)
    row_hit = (
        (row_place[None, :] == jnp.arange(span, dtype=jnp.int32)[:, None]) & live[None, :]
    ).astype(jnp.float32)
    col_hit = (
        (col_place[None, :] == jnp.arange(colspan, dtype=jnp.int32)[:, None]) & mirror[None, :]
    ).astype(jnp.float32)
    row_part = jnp.einsum("at,vti->vai", row_hit, down, precision=lax.Precision.HIGHEST).reshape(
        vlocal, span * tile
    )
    col_part = jnp.einsum("at,vti->vai", col_hit, upper, precision=lax.Precision.HIGHEST).reshape(
        vlocal, colspan * tile
    )
    row_whole = lax.psum(row_part, "col")
    col_whole = lax.psum(col_part, "row")
    row_share = lax.dynamic_slice_in_dim(row_whole, lax.axis_index("col") * width, width, 1)
    col_share = lax.dynamic_slice_in_dim(col_whole, lax.axis_index("row") * width, width, 1)
    image = row_share + col_share
    every_vector = lax.all_gather(vectors, "vec", axis=0, tiled=True)
    partial_gram = jnp.dot(
        every_vector.astype(jnp.float32), image.T, precision=lax.Precision.HIGHEST
    )
    gram = lax.psum(partial_gram, ("row", "col")) / math.sqrt(width * nrow * ncol)
    return (image.astype(jnp.bfloat16), gram)


def solution(mesh):
    return jax.shard_map(
        shards,
        mesh=mesh,
        in_specs=(
            P("vec", ("row", "col")),
            P("row", "col", None, None, None),
            P("row", "col", None),
            P("row", "col", None),
            P("row", "col"),
        ),
        out_specs=(P("vec", ("row", "col")), P(None, "vec")),
        check_vma=False,
    )
```

profile of v0, /device:TPU:8, one launch (start us, length us, event | category | flops | bytes accessed | tf_op | source)
XLA Modules:
  0.0 527.4 jit_solution(8425430569256399796)
XLA Ops:
  7.2 0.0 copy-start.1
  7.2 0.0 copy-start.2
  7.2 0.0 all-reduce.5.cloned.1.call-start
  7.2 28.5 %all_gather.10 = bf16[8,8192]{1,0:T(8,128)(2,1)S(1)} all-gather(bf16[8,1024]{1,0:T(8,128)(2,1)} %param.5), channel_id=1, replica_groups=mesh['row'=16,'col'=8,'vec'=2] {'col'}, dimensions={1}, use_global_device_ids=true | all-gather | bytes 147456 | tf_op jit(solution)/shard_map/all_gather | solution.py:16
  35.8 0.7 compare_select_fusion
  36.5 0.7 compare_and_fusion.1
  37.2 0.8 gather_fusion.1
  38.0 0.0 copy-start
  38.0 4.7 fusion
  42.7 0.4 copy.9
  43.8 0.0 copy-done.1
  43.8 0.0 copy-done.2
  43.8 0.6 convolution_bitcast_fusion
  44.5 0.2 copy.7
  44.7 1.1 copy.18
  45.8 0.0 all-reduce.5.cloned.1.call-update
  45.8 0.0 all-reduce.3.cloned.1.call-start
  45.9 0.0 copy-done
  45.9 20.7 %all_gather.9 = bf16[8,16384]{1,0:T(8,128)(2,1)S(1)} all-gather(bf16[8,1024]{1,0:T(8,128)(2,1)S(1)} %copy-done), channel_id=1, replica_groups=mesh['row'=16,'col'=8,'vec'=2] {'row'}, dimensions={1}, use_global_device_ids=true | all-gather | bytes 278528 | tf_op jit(solution)/shard_map/all_gather | solution.py:17
  66.6 0.8 gather_fusion
  67.4 6.8 %fusion.2 = f32[256,8,128]{2,1,0:T(8,128)S(1)} fusion(bf16[1,1,256,128,128]{4,3,2,1,0:T(8,128)(2,1)} %param.6, bf16[256,8,128]{2,1,0:T(8,128)(2,1)S(1)} %gather_fusion, pred[256]{0:T(512)(128)(4,1)S(1)} %get-tuple-element.2), kind=kOutput, calls=%fused_computation.4 | convolution fusion | flops 67371008 | bytes 9961728 | tf_op jit(solution)/shard_map/tij,vtj->vti/dot_general | solution.py:31
  74.2 0.6 convolution_bitcast_fusion.1
  74.8 0.9 copy.19
  75.7 0.0 all-reduce.3.cloned.1.call-update
  75.7 5.9 %all_gather.11 = bf16[16,1024]{1,0:T(8,128)(2,1)S(1)} all-gather(bf16[8,1024]{1,0:T(8,128)(2,1)S(1)} %copy-done), channel_id=1, replica_groups=mesh['row'=16,'col'=8,'vec'=2] {'vec'}, dimensions={0}, use_global_device_ids=true | all-gather | bytes 49152 | tf_op jit(solution)/shard_map/all_gather | solution.py:50
  81.7 77.3 %all-reduce.5.cloned.1.call-done = f32[8,16384]{1,0:T(8,128)} async-done(((f32[8,16384]{1,0:T(8,128)}), f32[8,16384]{1,0:T(8,128)}) %all-reduce.5.cloned.1.call-update) | async-done | bytes 524304 | tf_op jit(solution)/shard_map/psum | solution.py:46
  159.0 79.9 %all-reduce.3.cloned.1.call-done = f32[8,8192]{1,0:T(8,128)} async-done(((f32[8,8192]{1,0:T(8,128)}), f32[8,8192]{1,0:T(8,128)}) %all-reduce.3.cloned.1.call-update) | async-done | bytes 262160 | tf_op jit(solution)/shard_map/psum | solution.py:45
  238.9 0.9 convolution_bitcast_fusion.2
  239.8 278.8 %psum.23 = f32[16,8]{0,1:T(8,128)S(1)} all-reduce(f32[16,8]{0,1:T(8,128)S(1)} %convolution_bitcast_fusion.2), channel_id=1, replica_groups=mesh['row'=16,'col'=8,'vec'=2] {'row','col'}, use_global_device_ids=true, to_apply=%region_2.3 | all-reduce | flops 128 | bytes 1024 | tf_op jit(solution)/shard_map/psum | solution.py:54
  518.6 0.6 broadcast_multiply_fusion
  519.2 1.4 fusion.25
  (5 shorter events, 0.1 us)
Async XLA Ops:
  7.2 36.6 %copy-start.1 = (s32[1,1,256]{2,1,0:T(1,128)S(1)}, s32[1,1,256]{2,1,0:T(1,128)}, u32[]{:S(2)}) copy-start(s32[1,1,256]{2,1,0:T(1,128)} %param.7) | copy-start | bytes 3076
  7.2 36.6 %copy-start.2 = (s32[1,1,256]{2,1,0:T(1,128)S(1)}, s32[1,1,256]{2,1,0:T(1,128)}, u32[]{:S(2)}) copy-start(s32[1,1,256]{2,1,0:T(1,128)} %param.8) | copy-start | bytes 3076
  7.2 151.8 %all-reduce.5.cloned.1.call-start = ((), (), s32[]{:S(2)}) async-start(), calls=%async_computation.1 | async-start | bytes 1048576 | tf_op jit(solution)/shard_map/psum | solution.py:46
  38.0 7.9 %copy-start = (bf16[8,1024]{1,0:T(8,128)(2,1)S(1)}, bf16[8,1024]{1,0:T(8,128)(2,1)}, u32[]{:S(2)}) copy-start(bf16[8,1024]{1,0:T(8,128)(2,1)} %param.5) | copy-start | bytes 49156
  45.8 193.1 %all-reduce.3.cloned.1.call-start = ((), (), s32[]{:S(2)}) async-start(), calls=%async_computation | async-start | bytes 524288 | tf_op jit(solution)/shard_map/psum | solution.py:45
Sparse Core Ops, SparseCore 0:
  45.9 113.0 all-reduce.4
  161.6 77.2 all-reduce.2
where the time goes:
time: 528 us; the launch traced here: 527 us
  blocking collectives  334 us (63%)
  waiting for transfers between devices  157 us (30%)
  between operations  14.8 us (3%)
  matrix products  13.7 us (3%)
    psum x1, blocking collectives, shards(): lax.psum(partial_gram, ('row', 'col')) / math.sqrt(width * nrow * ncol)  279 us
    psum x1, waiting for transfers between devices, shards(): row_whole = lax.psum(row_part, 'col')  79.9 us
    psum x1, waiting for transfers between devices, shards(): col_whole = lax.psum(col_part, 'row')  77.3 us
    all_gather x1, blocking collectives, shards(): row_x = lax.all_gather(vectors, 'col', axis=1, tiled=True)  28.5 us
    all_gather x1, blocking collectives, shards(): col_x = lax.all_gather(vectors, 'row', axis=1, tiled=True)  20.7 us
  transfers between devices with their start and end apart: 2, of which 2 were waited for; matrix products, arithmetic and copies ran while one was open for 2% of the time, Pallas kernels for 0%

commit v1 on v0

--- a/solution.py
+++ b/solution.py
@@ -42,7 +42,7 @@
     col_part = jnp.einsum("at,vti->vai", col_hit, upper, precision=lax.Precision.HIGHEST).reshape(
         vlocal, colspan * tile
     )
-    row_whole = lax.psum(row_part, "col")
+    row_whole = jnp.sum(lax.all_gather(row_part, "col"), axis=0)
     col_whole = lax.psum(col_part, "row")
     row_share = lax.dynamic_slice_in_dim(row_whole, lax.axis_index("col") * width, width, 1)
     col_share = lax.dynamic_slice_in_dim(col_whole, lax.axis_index("row") * width, width, 1)

time: 528 us -> 478 us (0.905)
  waiting for transfers between devices: 157 us -> 100 us
    psum x1 -> x0, waiting for transfers between devices: 79.9 us -> none  [shards(): row_whole = lax.psum(row_part, 'col')]
    psum x1, waiting for transfers between devices: 77.3 us -> 91 us  [shards(): col_whole = lax.psum(col_part, 'row')]
    all_gather x0 -> x1, waiting for transfers between devices: none -> 9.42 us  [shards(): row_whole = jnp.sum(lax.all_gather(row_part, 'col'), axis=0)]
where the time goes in v1:
time: 478 us; the launch traced here: 473 us
  blocking collectives  334 us (70%)
  waiting for transfers between devices  100 us (21%)
  between operations  16.2 us (3%)
  matrix products  14.1 us (3%)
  other arithmetic  5.12 us (1%)
    psum x1, blocking collectives, shards(): lax.psum(partial_gram, ('row', 'col')) / math.sqrt(width * nrow * ncol)  277 us
    psum x1, waiting for transfers between devices, shards(): col_whole = lax.psum(col_part, 'row')  91 us
    all_gather x1, blocking collectives, shards(): row_x = lax.all_gather(vectors, 'col', axis=1, tiled=True)  29.2 us
    all_gather x1, blocking collectives, shards(): col_x = lax.all_gather(vectors, 'row', axis=1, tiled=True)  20.9 us
  transfers between devices with their start and end apart: 2, of which 2 were waited for; matrix products, arithmetic and copies ran while one was open for 2% of the time, Pallas kernels for 0%

profile of v1, /device:TPU:8, one launch (start us, length us, event | category | flops | bytes accessed | tf_op | source)
XLA Modules:
  0.0 473.5 jit_solution(6371742804245376323)
XLA Ops:
  8.0 0.0 copy-start
  8.0 0.0 copy-start.1
  8.0 0.0 all-gather.2.cloned.1.call-start
  8.7 20.9 %all_gather.12 = bf16[8,16384]{1,0:T(8,128)(2,1)S(1)} all-gather(bf16[8,1024]{1,0:T(8,128)(2,1)} %param.5), channel_id=1, replica_groups=mesh['row'=16,'col'=8,'vec'=2] {'row'}, dimensions={1}, use_global_device_ids=true | all-gather | bytes 278528 | tf_op jit(solution)/shard_map/all_gather | solution.py:17
  29.6 0.7 compare_select_fusion.1
  30.4 0.8 gather_fusion
  31.2 0.7 compare_and_fusion.1
  31.9 6.8 %fusion.4 = f32[8,256,128]{2,0,1:T(8,128)S(1)} fusion(bf16[1,1,256,128,128]{4,3,2,1,0:T(8,128)(2,1)} %param.6, bf16[256,8,128]{2,1,0:T(8,128)(2,1)S(1)} %gather_fusion, pred[256]{0:T(512)(128)(4,1)S(1)} %get-tuple-element.8), kind=kOutput, calls=%fused_computation.6 | convolution fusion | flops 67371008 | bytes 9961728 | tf_op jit(solution)/shard_map/tij,vtj->vti/dot_general | solution.py:31
  38.7 0.6 convolution_bitcast_fusion.1
  39.3 0.8 all_gather_reshape.3
  40.1 0.0 all-gather.2.cloned.1.call-update
  40.1 0.0 all-reduce.2.cloned.1.call-start
  40.2 0.0 copy-done
  40.2 29.2 %all_gather.14 = bf16[8,8192]{1,0:T(8,128)(2,1)S(1)} all-gather(bf16[8,1024]{1,0:T(8,128)(2,1)S(1)} %copy-done), channel_id=1, replica_groups=mesh['row'=16,'col'=8,'vec'=2] {'col'}, dimensions={1}, use_global_device_ids=true | all-gather | bytes 147456 | tf_op jit(solution)/shard_map/all_gather | solution.py:16
  69.4 0.0 copy-done.1
  69.4 0.8 gather_fusion.1
  70.2 4.8 %fusion.7 = f32[8,256,128]{2,0,1:T(8,128)S(1)} fusion(bf16[1,1,256,128,128]{4,3,2,1,0:T(8,128)(2,1)} %param.6, bf16[256,8,128]{2,1,0:T(8,128)(2,1)S(1)} %gather_fusion.1, pred[256]{0:T(512)(128)(4,1)S(1)} %get-tuple-element.4), kind=kOutput, calls=%fused_computation.7 | convolution fusion | flops 67371008 | bytes 9961728 | tf_op jit(solution)/shard_map/tij,vti->vtj/dot_general | solution.py:32
  75.0 1.0 convolution_bitcast_fusion
  76.0 0.2 copy.10
  76.2 1.1 copy.17
  77.3 0.0 all-reduce.2.cloned.1.call-update
  77.4 6.8 %all_gather.15 = bf16[16,1024]{1,0:T(8,128)(2,1)S(1)} all-gather(bf16[8,1024]{1,0:T(8,128)(2,1)S(1)} %copy-done), channel_id=1, replica_groups=mesh['row'=16,'col'=8,'vec'=2] {'vec'}, dimensions={0}, use_global_device_ids=true | all-gather | bytes 49152 | tf_op jit(solution)/shard_map/all_gather | solution.py:50
  84.2 9.4 %all-gather.2.cloned.1.call-done = f32[8,8,8192]{2,1,0:T(8,128)} async-done(((f32[1,8,8192]{2,1,0:T(8,128)}), f32[8,8,8192]{2,1,0:T(8,128)}) %all-gather.2.cloned.1.call-update) | async-done | bytes 2097168 | tf_op jit(solution)/shard_map/all_gather | solution.py:45
  93.6 1.7 reduce_sum.9
  95.3 91.0 %all-reduce.2.cloned.1.call-done = f32[8,16384]{1,0:T(8,128)} async-done(((f32[8,16384]{1,0:T(8,128)}), f32[8,16384]{1,0:T(8,128)}) %all-reduce.2.cloned.1.call-update) | async-done | bytes 524304 | tf_op jit(solution)/shard_map/psum | solution.py:46
  186.3 0.9 convolution_bitcast_fusion.2
  187.2 276.8 %psum.15 = f32[16,8]{0,1:T(8,128)S(1)} all-reduce(f32[16,8]{0,1:T(8,128)S(1)} %convolution_bitcast_fusion.2), channel_id=1, replica_groups=mesh['row'=16,'col'=8,'vec'=2] {'row','col'}, use_global_device_ids=true, to_apply=%region_2.3 | all-reduce | flops 128 | bytes 1024 | tf_op jit(solution)/shard_map/psum | solution.py:54
  464.0 0.6 broadcast_multiply_fusion
  464.6 1.4 fusion.30
  (4 shorter events, 0.0 us)
Async XLA Ops:
  8.0 32.2 %copy-start = (bf16[8,1024]{1,0:T(8,128)(2,1)S(1)}, bf16[8,1024]{1,0:T(8,128)(2,1)}, u32[]{:S(2)}) copy-start(bf16[8,1024]{1,0:T(8,128)(2,1)} %param.5) | copy-start | bytes 49156
  8.0 61.4 %copy-start.1 = (s32[1,1,256]{2,1,0:T(1,128)S(1)}, s32[1,1,256]{2,1,0:T(1,128)}, u32[]{:S(2)}) copy-start(s32[1,1,256]{2,1,0:T(1,128)} %param.7) | copy-start | bytes 3076
  8.0 85.6 %all-gather.2.cloned.1.call-start = ((), (), s32[]{:S(2)}) async-start(), calls=%async_computation | async-start | bytes 2359296 | tf_op jit(solution)/shard_map/all_gather | solution.py:45
  40.1 146.2 %all-reduce.2.cloned.1.call-start = ((), (), s32[]{:S(2)}) async-start(), calls=%async_computation.1 | async-start | bytes 1048576 | tf_op jit(solution)/shard_map/psum | solution.py:46
Sparse Core Ops, SparseCore 0:
  40.3 53.2 all-gather.1
Sparse Core Ops, SparseCore 1:
  77.5 108.8 all-reduce.1
